TPU v7x, 32 devices: a whole 2x2x4 slice. The times are simulated.
32 devices in a mesh: seq: 16 (over z, y, core), tp: 2 (over x).
Axes of the slice: x: 2, y: 2, z: 4, core: 2. Of those that a mesh axis runs over, the one named last changes fastest.
Arguments:
- layer_in: bfloat16 [32768, 768], P(('seq', 'tp')), may hold values from -6 to 6
- skip_values: bfloat16 [32768, 384], P('seq', 'tp'), may hold values from -6 to 6
- block_slot: int32 [16, 8], replicated, may hold values from 0 to 3, as said below
- doc_lengths: int32 [32, 4], replicated, may hold values from 1 to 512, 1024 in all within a row
- gain_attention: float32 [768], replicated, may hold values from 0.5 to 1.5
- shift_attention: float32 [768], replicated, may hold values from -1.5 to 1.5
- query_weight: bfloat16 [768, 768], P(None, 'tp'), may hold values from -0.21875 to 0.21875
- query_bias: float32 [768], P('tp'), may hold values from -1.5 to 1.5
- key_weight: bfloat16 [768, 768], P(None, 'tp'), may hold values from -0.21875 to 0.21875
- value_weight: bfloat16 [768, 384], P(None, 'tp'), may hold values from -0.21875 to 0.21875
- value_bias: float32 [384], P('tp'), may hold values from -1.5 to 1.5
- out_weight: bfloat16 [768, 768], P('tp'), may hold values from -1.75 to 1.75
- out_bias: float32 [768], replicated, may hold values from -1.5 to 1.5
- gain_feed: float32 [768], replicated, may hold values from 0.5 to 1.5
- shift_feed: float32 [768], replicated, may hold values from -1.5 to 1.5
- up_weight: bfloat16 [768, 3072], P(None, 'tp'), may hold values from -0.21875 to 0.21875
- up_bias: float32 [3072], P('tp'), may hold values from -1.5 to 1.5
- down_weight: bfloat16 [3072, 768], P('tp'), may hold values from -0.109375 to 0.109375
- down_bias: float32 [768], replicated, may hold values from -1.5 to 1.5
- out_grad: bfloat16 [32768, 768], P(('seq', 'tp')), may hold values from -6 to 6
Outputs:
- layer_out: bfloat16 [32768, 768], P(('seq', 'tp'))
- input_grad: float32 [32768, 768], P(('seq', 'tp'))
- skip_grad: float32 [32768, 384], P('seq', 'tp')
- grad_gain_attention: float32 [768], replicated
- grad_shift_attention: float32 [768], replicated
- grad_query_weight: float32 [768, 768], P(None, 'tp')
- grad_query_bias: float32 [768], P('tp')
- grad_key_weight: float32 [768, 768], P(None, 'tp')
- grad_value_weight: float32 [768, 384], P(None, 'tp')
- grad_value_bias: float32 [384], P('tp')
- grad_out_weight: float32 [768, 768], P('tp')
- grad_out_bias: float32 [768], replicated
- grad_gain_feed: float32 [768], replicated
- grad_shift_feed: float32 [768], replicated
- grad_up_weight: float32 [768, 3072], P(None, 'tp')
- grad_up_bias: float32 [3072], P('tp')
- grad_down_weight: float32 [3072, 768], P('tp')
- grad_down_bias: float32 [768], replicated
Inputs may be any that keep to these rules, and one draw needn't show every extreme that they name: `block_slot`: for each group of 4 consecutive rows (the seq indices that hold one set of sequences) and each column, the entries are a permutation of 0 to 3. `doc_lengths`: each row gives the lengths of the documents of one sequence in order; a row sums to 1024.
All inputs are finite; a program needn't handle non-finite values.
Results may differ from a plain program's by a relative error of at most 0.015.
Values may be sent and summed in bfloat16 or wider, within the bound.
No kernel may reach another device: no remote copies, remote signals or barrier semaphores. Data moves between devices by JAX's collectives and lax.ppermute only.
A program may use at most 320 MiB of HBM per device.

v0:
```python
from functools import partial
from functools import reduce
import jax
import jax.numpy as jnp
from jax import lax
from jax.sharding import PartitionSpec as P

HEAD = 64
SEQ_LEN = 1024
BLOCK = 256
EPSILON = 1e-05


def from_partner(block, axis, apart):
    count = lax.axis_size(axis)
    route = []
    for low in range(count):
        high = low | 1 << apart
        if high != low and high < count:
            route += [(low, high), (high, low)]
    return lax.ppermute(block, axis, route)


def product(left, right):
    return jnp.dot(left, right, preferred_element_type=jnp.float32)


def product_rt(left, right):
    return lax.dot_general(
        left, right, (((1,), (1,)), ((), ())), preferred_element_type=jnp.float32
    )


def product_lt(left, right):
    return lax.dot_general(
        left, right, (((0,), (0,)), ((), ())), preferred_element_type=jnp.float32
    )


def norm_rows(rows, gain, shift):
    centred = rows - jnp.mean(rows, axis=-1, keepdims=True)
    inverse = lax.rsqrt(jnp.mean(centred * centred, axis=-1, keepdims=True) + EPSILON)
    scaled = centred * inverse
    return (scaled * gain + shift, scaled, inverse)


def norm_back(grad_out, scaled, inverse, gain):
    grad_scaled = grad_out * gain
    first_mean = jnp.mean(grad_scaled, axis=-1, keepdims=True)
    second_mean = jnp.mean(grad_scaled * scaled, axis=-1, keepdims=True)
    return inverse * (grad_scaled - first_mean - scaled * second_mean)


def block_places(slots, bounds):
    within = jnp.arange(BLOCK, dtype=jnp.int32)
    places = slots[:, None] * BLOCK + within[None, :]
    doc_ids = jnp.sum((places[:, :, None] >= bounds[:, None, :]).astype(jnp.int32), axis=2)
    return (places, doc_ids)


def swap_blocks(held, level):
    return from_partner(held, "seq", level)


def swap_grads(held, level):
    return from_partner(held.astype(jnp.bfloat16), "seq", level).astype(held.dtype)


def per_device(
    layer_in,
    skip_values,
    block_slot,
    doc_lengths,
    gain_attention,
    shift_attention,
    query_weight,
    query_bias,
    key_weight,
    value_weight,
    value_bias,
    out_weight,
    out_bias,
    gain_feed,
    shift_feed,
    up_weight,
    up_bias,
    down_weight,
    down_bias,
    out_grad,
):
    seq_span = SEQ_LEN // BLOCK
    span_levels = seq_span.bit_length() - 1
    level_order = list(range(span_levels))
    seq_batch = skip_values.shape[0] // BLOCK
    rows_all = seq_batch * BLOCK
    heads_here = query_weight.shape[1] // HEAD
    fresh_cols = value_weight.shape[1]
    score_scale = HEAD ** (-0.5)
    my_index = lax.axis_index("seq")
    my_member = my_index % seq_span
    group_id = my_index // seq_span
    lengths_here = lax.dynamic_slice_in_dim(doc_lengths, group_id * seq_batch, seq_batch, 0)
    bounds = jnp.cumsum(lengths_here, axis=1)[:, :-1]

    def places_of(member_id):
        slots = lax.dynamic_index_in_dim(
            block_slot, group_id * seq_span + member_id, 0, keepdims=False
        )
        return block_places(slots, bounds)

    own_places, own_docs = places_of(my_member)

    def visible_of(member_id):
        key_places, key_docs = places_of(member_id)
        return (key_places[:, None, :] <= own_places[:, :, None]) & (
            key_docs[:, None, :] == own_docs[:, :, None]
        )

    def heads_view(rows):
        return rows.reshape(seq_batch, BLOCK, heads_here, HEAD)

    input_float = layer_in.astype(jnp.float32)
    first_norm, first_scaled, first_inverse = norm_rows(
        input_float, gain_attention, shift_attention
    )
    first_rows = lax.all_gather(first_norm.astype(jnp.bfloat16), "tp", axis=0, tiled=True)
    queries = (product(first_rows, query_weight) + query_bias).astype(jnp.bfloat16)
    keys_here = product(first_rows, key_weight).astype(jnp.bfloat16)
    fresh = (product(first_rows, value_weight) + value_bias).astype(jnp.bfloat16)
    values_here = jnp.concatenate([fresh, skip_values], axis=1)
    query_heads = heads_view(queries)
    sources = [(heads_view(keys_here), heads_view(values_here), visible_of(my_member))]
    held = jnp.stack([keys_here, values_here])[None]
    for level in level_order:
        held = jnp.concatenate([held, swap_blocks(held, level)], axis=0)
    for slot in range(1, seq_span):
        partner = 0
        for step in range(span_levels):
            partner = partner + ((slot >> step & 1) << level_order[step])
        sources.append(
            (
                heads_view(held[slot, 0]),
                heads_view(held[slot, 1]),
                visible_of(jnp.bitwise_xor(my_member, partner)),
            )
        )

    def scores_of(key_heads, seen_mask):
        raw = (
            jnp.einsum(
                "bqhe,bkhe->bhqk", query_heads, key_heads, preferred_element_type=jnp.float32
            )
            * score_scale
        )
        return jnp.where(seen_mask[:, None], raw, -jnp.inf)

    score_list = [scores_of(key_heads, seen_mask) for key_heads, value_heads, seen_mask in sources]
    row_max = reduce(jnp.maximum, [jnp.max(scores, axis=-1) for scores in score_list])
    row_total = reduce(
        jnp.add, [jnp.sum(jnp.exp(scores - row_max[..., None]), axis=-1) for scores in score_list]
    )
    log_total = row_max + jnp.log(row_total)
    attended = reduce(
        jnp.add,
        [
            jnp.einsum(
                "bhqk,bkhe->bqhe",
                jnp.exp(scores - log_total[..., None]).astype(jnp.bfloat16),
                source[1],
                preferred_element_type=jnp.float32,
            )
            for scores, source in zip(score_list, sources)
        ],
    )
    attended_rows = attended.reshape(rows_all, heads_here * HEAD).astype(jnp.bfloat16)
    middle = (
        input_float
        + lax.psum_scatter(
            product(attended_rows, out_weight).astype(jnp.bfloat16),
            "tp",
            scatter_dimension=0,
            tiled=True,
        ).astype(jnp.float32)
        + out_bias
    )
    second_norm, second_scaled, second_inverse = norm_rows(middle, gain_feed, shift_feed)
    second_rows = lax.all_gather(second_norm.astype(jnp.bfloat16), "tp", axis=0, tiled=True)
    hidden = product(second_rows, up_weight) + up_bias
    activated, gelu_back = jax.vjp(partial(jax.nn.gelu, approximate=True), hidden)
    activated_low = activated.astype(jnp.bfloat16)
    feed_out = lax.psum_scatter(
        product(activated_low, down_weight).astype(jnp.bfloat16),
        "tp",
        scatter_dimension=0,
        tiled=True,
    ).astype(jnp.float32)
    layer_out = (middle + feed_out + down_bias).astype(jnp.bfloat16)
    grad_output = out_grad.astype(jnp.float32)
    grad_down_bias = jnp.sum(grad_output, axis=0)
    grad_rows_all = lax.all_gather(out_grad, "tp", axis=0, tiled=True)
    grad_down_weight = product_lt(activated_low, grad_rows_all)
    grad_hidden = gelu_back(product_rt(grad_rows_all, down_weight))[0]
    grad_up_bias = jnp.sum(grad_hidden, axis=0)
    hidden_low = grad_hidden.astype(jnp.bfloat16)
    grad_up_weight = product_lt(second_rows, hidden_low)
    second_grad = lax.psum_scatter(
        product_rt(hidden_low, up_weight).astype(jnp.bfloat16),
        "tp",
        scatter_dimension=0,
        tiled=True,
    ).astype(jnp.float32)
    grad_gain_feed = jnp.sum(second_grad * second_scaled, axis=0)
    grad_shift_feed = jnp.sum(second_grad, axis=0)
    middle_grad = grad_output + norm_back(second_grad, second_scaled, second_inverse, gain_feed)
    grad_out_bias = jnp.sum(middle_grad, axis=0)
    middle_rows = lax.all_gather(middle_grad.astype(jnp.bfloat16), "tp", axis=0, tiled=True)
    grad_out_weight = product_lt(attended_rows, middle_rows)
    grad_heads = heads_view(product_rt(middle_rows, out_weight).astype(jnp.bfloat16))
    prob_list = []
    dprob_list = []
    for key_heads, value_heads, seen_mask in sources:
        prob_list.append(jnp.exp(scores_of(key_heads, seen_mask) - log_total[..., None]))
        dprob_list.append(
            jnp.einsum(
                "bqhe,bkhe->bhqk", grad_heads, value_heads, preferred_element_type=jnp.float32
            )
        )
    delta = reduce(
        jnp.add, [jnp.sum(probs * dprobs, axis=-1) for probs, dprobs in zip(prob_list, dprob_list)]
    )
    query_parts = []
    pair_grads = []
    for probs, dprobs, source in zip(prob_list, dprob_list, sources):
        dscores = (probs * (dprobs - delta[..., None])).astype(jnp.bfloat16)
        query_parts.append(
            jnp.einsum("bhqk,bkhe->bqhe", dscores, source[0], preferred_element_type=jnp.float32)
            * score_scale
        )
        key_part = (
            jnp.einsum("bhqk,bqhe->bkhe", dscores, query_heads, preferred_element_type=jnp.float32)
            * score_scale
        )
        value_part = jnp.einsum(
            "bhqk,bqhe->bkhe",
            probs.astype(jnp.bfloat16),
            grad_heads,
            preferred_element_type=jnp.float32,
        )
        pair_grads.append(jnp.stack([key_part, value_part]))
    held_grads = jnp.stack(pair_grads)
    for step in reversed(range(span_levels)):
        half = 1 << step
        held_grads = held_grads[:half] + swap_grads(held_grads[half:], level_order[step])
    pair_total = held_grads[0]
    query_grad = reduce(jnp.add, query_parts).reshape(rows_all, heads_here * HEAD)
    key_grad = pair_total[0].reshape(rows_all, heads_here * HEAD)
    value_grad = pair_total[1].reshape(rows_all, heads_here * HEAD)
    fresh_grad = value_grad[:, :fresh_cols]
    skip_grad = value_grad[:, fresh_cols:]
    grad_query_bias = jnp.sum(query_grad, axis=0)
    grad_value_bias = jnp.sum(fresh_grad, axis=0)
    query_low = query_grad.astype(jnp.bfloat16)
    key_low = key_grad.astype(jnp.bfloat16)
    fresh_low = fresh_grad.astype(jnp.bfloat16)
    grad_query_weight = product_lt(first_rows, query_low)
    grad_key_weight = product_lt(first_rows, key_low)
    grad_value_weight = product_lt(first_rows, fresh_low)
    first_terms = (
        product_rt(query_low, query_weight)
        + product_rt(key_low, key_weight)
        + product_rt(fresh_low, value_weight)
    )
    first_grad = lax.psum_scatter(
        first_terms.astype(jnp.bfloat16), "tp", scatter_dimension=0, tiled=True
    ).astype(jnp.float32)
    grad_gain_attention = jnp.sum(first_grad * first_scaled, axis=0)
    grad_shift_attention = jnp.sum(first_grad, axis=0)
    input_grad = middle_grad + norm_back(first_grad, first_scaled, first_inverse, gain_attention)
    (
        grad_query_weight,
        grad_query_bias,
        grad_key_weight,
        grad_value_weight,
        grad_value_bias,
        grad_out_weight,
        grad_up_weight,
        grad_up_bias,
        grad_down_weight,
    ) = lax.psum(
        (
            grad_query_weight,
            grad_query_bias,
            grad_key_weight,
            grad_value_weight,
            grad_value_bias,
            grad_out_weight,
            grad_up_weight,
            grad_up_bias,
            grad_down_weight,
        ),
        "seq",
    )
    (
        grad_gain_attention,
        grad_shift_attention,
        grad_gain_feed,
        grad_shift_feed,
        grad_out_bias,
        grad_down_bias,
    ) = lax.psum(
        (
            grad_gain_attention,
            grad_shift_attention,
            grad_gain_feed,
            grad_shift_feed,
            grad_out_bias,
            grad_down_bias,
        ),
        ("seq", "tp"),
    )
    return (
        layer_out,
        input_grad,
        skip_grad,
        grad_gain_attention,
        grad_shift_attention,
        grad_query_weight,
        grad_query_bias,
        grad_key_weight,
        grad_value_weight,
        grad_value_bias,
        grad_out_weight,
        grad_out_bias,
        grad_gain_feed,
        grad_shift_feed,
        grad_up_weight,
        grad_up_bias,
        grad_down_weight,
        grad_down_bias,
    )


def solution(mesh):
    return jax.shard_map(
        per_device,
        mesh=mesh,
        in_specs=(
            P(("seq", "tp"), None),
            P("seq", "tp"),
            P(),
            P(),
            P(),
            P(),
            P(None, "tp"),
            P("tp"),
            P(None, "tp"),
            P(None, "tp"),
            P("tp"),
            P("tp", None),
            P(),
            P(),
            P(),
            P(None, "tp"),
            P("tp"),
            P("tp", None),
            P(),
            P(("seq", "tp"), None),
        ),
        out_specs=(
            P(("seq", "tp"), None),
            P(("seq", "tp"), None),
            P("seq", "tp"),
            P(),
            P(),
            P(None, "tp"),
            P("tp"),
            P(None, "tp"),
            P(None, "tp"),
            P("tp"),
            P("tp", None),
            P(),
            P(),
            P(),
            P(None, "tp"),
            P("tp"),
            P("tp", None),
            P(),
        ),
        check_vma=False,
    )
```

profile of v0, /device:TPU:0, one launch (start us, length us, event | category | flops | bytes accessed | tf_op | source)
XLA Modules:
  0.0 1259.1 jit_solution(5588381925399778991)
XLA Ops:
  13.7 47.7 %all-gather.5.cloned.1.call-done = bf16[2048,768]{1,0:T(8,128)(2,1)} async-done(((bf16[1024,768]{1,0:T(8,128)(2,1)}), bf16[2048,768]{1,0:T(8,128)(2,1)}) %all-gather.5.cloned.1.call-update) | async-done | bytes 3145744 | tf_op jit(solution)/shard_map/all_gather | solution.py:126
  61.4 3.1 fusion.40
  69.7 5.7 collective-permute-done
  75.3 3.5 pad_maximum_fusion
  81.2 4.5 compare_and_fusion.2
  87.4 4.0 add_convert_fusion.4
  96.6 6.0 fusion.6
  103.8 6.0 fusion.7
  109.8 107.2 %collective-permute-done.1 = bf16[2,2,2048,384]{2,3,1,0:T(8,128)(2,1)} collective-permute-done((bf16[2,2,2048,384]{2,3,1,0:T(8,128)(2,1)}, bf16[2,2,2048,384]{2,3,1,0:T(8,128)(2,1)}, u32[]{:S(2)}, u32[]{:S(2)}) %collective-permute-start.1) | collective-permute-done | bytes 6291488 | tf_op jit(solution)/shard_map/ppermute | solution.py:21
  217.0 3.5 fusion.105
  224.0 6.5 fusion.8
  230.5 2.9 fusion.9
  233.4 20.6 %exponential_reduce_fusion.2 = (f32[8,6,256]{2,1,0:T(8,128)S(1)}, f32[8,6,256]{2,1,0:T(8,128)S(1)}, f32[8,6,256]{2,1,0:T(8,128)S(1)}, f32[8,6,256]{2,1,0:T(8,128)S(1)}) fusion(f32[8,6,256,256]{2,3,1,0:T(8,128)} %get-tuple-element.86, f32[8,6,256]{2,1,0:T(8,128)S(1)} %maximum_maximum_fusion, pred[8,256,256]{1,2,0:T(8,128)(4,1)S(1)} %copy-done.24, ...), kind=kLoop, calls=%fused_computation.24 | loop fusion | flops 50282496 | bytes 52674560 | tf_op jit(solution)/shard_map/reduce_sum | solution.py:160
  254.1 9.3 fusion.51
  263.3 9.3 fusion.55
  272.6 9.2 fusion.59
  281.9 7.9 fusion.45
  293.9 3.5 convolution_convert_fusion
  297.5 43.4 %reduce-scatter.5.cloned.1.call-done = bf16[1024,768]{1,0:T(8,128)(2,1)} async-done(((bf16[2048,768]{1,0:T(8,128)(2,1)}), bf16[1024,768]{1,0:T(8,128)(2,1)}) %reduce-scatter.5.cloned.1.call-update) | async-done | bytes 1572880 | tf_op jit(solution)/shard_map/reduce_scatter | solution.py:178
  340.9 2.6 fusion.76
  347.3 44.5 %all-gather.7.cloned.1.call-done = bf16[2048,768]{1,0:T(8,128)(2,1)} async-done(((bf16[1024,768]{1,0:T(8,128)(2,1)}), bf16[2048,768]{1,0:T(8,128)(2,1)}) %all-gather.7.cloned.1.call-update) | async-done | bytes 3145744 | tf_op jit(solution)/shard_map/all_gather | solution.py:187
  391.8 13.3 %multiply_convert_fusion.4 = (bf16[2048,1536]{1,0:T(8,128)(2,1)}, f32[2048,1536]{1,0:T(8,128)}) fusion(f32[1536]{0:T(1024)S(1)} %copy-done.80, bf16[2048,768]{1,0:T(8,128)(2,1)} %all-gather.7.cloned.1.call-done, bf16[768,1536]{1,0:T(8,128)(2,1)S(1)} %copy-done), kind=kOutput, calls=%fused_computation.17 | convolution fusion | flops 4863295488 | bytes 24385536 | tf_op jit(solution)/shard_map/dot_general | solution.py:25
  405.1 33.1 %all-gather.9.cloned.1.call-done = bf16[2048,768]{1,0:T(8,128)(2,1)} async-done(((bf16[1024,768]{1,0:T(8,128)(2,1)}), bf16[2048,768]{1,0:T(8,128)(2,1)}) %all-gather.9.cloned.1.call-update) | async-done | bytes 3145744 | tf_op jit(solution)/shard_map/all_gather | solution.py:200
  438.2 17.5 %fusion.107 = (f32[1536]{0:T(1024)}, bf16[2048,1536]{1,0:T(8,128)(2,1)S(1)}) fusion(f32[2048,1536]{1,0:T(8,128)} %get-tuple-element.88, f32[1536]{0:T(1024)S(1)} %copy-done.80, bf16[2048,768]{1,0:T(8,128)(2,1)} %all-gather.9.cloned.1.call-done, bf16[1536,768]{1,0:T(8,128)(2,1)} %param.37), kind=kOutput, calls=%fused_computation.199 | convolution fusion | flops 4901042688 | bytes 24391680 | tf_op jit(solution)/shard_map/dot_general | solution.py:29
  458.3 6.4 convolution_convert_fusion.1
  466.4 9.6 convolution_convert_fusion.2
  476.1 32.2 %reduce-scatter.9.cloned.1.call-done = bf16[1024,768]{1,0:T(8,128)(2,1)} async-done(((bf16[2048,768]{1,0:T(8,128)(2,1)}), bf16[1024,768]{1,0:T(8,128)(2,1)}) %reduce-scatter.9.cloned.1.call-update) | async-done | bytes 1572880 | tf_op jit(solution)/shard_map/reduce_scatter | solution.py:206
  508.3 4.1 fusion.35
  512.3 42.0 %reduce-scatter.7.cloned.1.call-done = bf16[1024,768]{1,0:T(8,128)(2,1)} async-done(((bf16[2048,768]{1,0:T(8,128)(2,1)}), bf16[1024,768]{1,0:T(8,128)(2,1)}) %reduce-scatter.7.cloned.1.call-update) | async-done | bytes 1572880 | tf_op jit(solution)/shard_map/reduce_scatter | solution.py:191
  554.3 5.6 fusion.104
  563.0 45.0 %all-gather.11.cloned.1.call-done = bf16[2048,768]{1,0:T(8,128)(2,1)} async-done(((bf16[1024,768]{1,0:T(8,128)(2,1)}), bf16[2048,768]{1,0:T(8,128)(2,1)}) %all-gather.11.cloned.1.call-update) | async-done | bytes 3145744 | tf_op jit(solution)/shard_map/all_gather | solution.py:216
  608.0 3.7 convolution_convert_fusion.3
  615.3 8.9 fusion.41
  624.2 9.0 fusion.42
  633.2 6.4 fusion.49
  639.6 6.4 fusion.46
  646.0 6.6 fusion.57
  652.6 36.6 %multiply_reduce_fusion.2 = (f32[8,6,256]{2,1,0:T(8,128)S(1)}, f32[8,6,256]{2,1,0:T(8,128)S(1)}, f32[8,6,256]{2,1,0:T(8,128)S(1)}, f32[8,6,256]{2,1,0:T(8,128)S(1)}, f32[8,6,256,256]{2,3,1,0:T(8,128)}) fusion(f32[8,6,256,256]{2,3,1,0:T(8,128)} %get-tuple-element.86, f32[8,6,256]{2,1,0:T(8,128)S(1)} %log_add_fusion, pred[8,256,256]{1,2,0:T(8,128)(4,1)S(1)} %copy-done.25, ...), kind=kOutput, calls=%fused_computation.15 | convolution fusion | flops 465518592 | bytes 106151936 | tf_op jit(solution)/shard_map/bqhe,bkhe->bhqk/dot_general | solution.py:224
  689.2 42.7 %multiply_convert_fusion.1 = (bf16[8,6,256,256]{2,3,1,0:T(8,128)(2,1)}, bf16[8,6,256,256]{2,3,1,0:T(8,128)(2,1)}, bf16[8,6,256,256]{2,3,1,0:T(8,128)(2,1)}, bf16[8,6,256,256]{2,3,1,0:T(8,128)(2,1)}) fusion(f32[8,6,256,256]{2,3,1,0:T(8,128)} %fusion.49, f32[8,6,256,256]{2,3,1,0:T(8,128)} %get-tuple-element.82, f32[8,6,256]{2,1,0:T(8,128)S(1)} %add_add_fusion, ...), kind=kLoop, calls=%fused_computation.10 | loop fusion | flops 75497472 | bytes 128024576 | tf_op jit(solution)/shard_map/convert_element_type | solution.py:234
  731.9 5.0 fusion.43
  742.8 6.5 pad_maximum_fusion.1
  750.8 6.6 multiply_bitcast_fusion
  757.4 4.5 convolution_bitcast_fusion
  761.9 6.5 maximum_bitcast_fusion.1
  768.4 6.6 multiply_bitcast_fusion.1
  775.1 4.5 convolution_bitcast_fusion.1
  779.5 2.8 maximum_bitcast_fusion
  782.4 104.5 %collective-permute-done.2 = bf16[2,2,8,256,6,64]{3,5,4,2,1,0:T(8,128)(2,1)} collective-permute-done((bf16[2,2,8,256,6,64]{3,5,4,2,1,0:T(8,128)(2,1)}, bf16[2,2,8,256,6,64]{3,5,4,2,1,0:T(8,128)(2,1)}, u32[]{:S(2)}, u32[]{:S(2)}) %collective-permute-start.2) | collective-permute-done | bytes 6291488 | tf_op jit(solution)/shard_map/ppermute | solution.py:21
  886.9 11.3 maximum_add_fusion
  898.2 5.1 slice.79
  906.3 2.7 fusion.72
  909.1 6.0 bitcast_convert_fusion
  918.4 5.7 slice_add_fusion
  934.4 3.7 add_convert_fusion
  938.2 10.0 fusion.37
  948.2 8.9 fusion.112
  959.5 2.9 fusion.109
  964.0 2.9 fusion.110
  969.1 3.3 slice_reduce_fusion
  972.5 64.0 %all-reduce.1 = (f32[384]{0:T(512)}, f32[192]{0:T(256)}, f32[1536]{0:T(1024)}) all-reduce(f32[384]{0:T(512)S(1)} %reduce_sum.290, f32[192]{0:T(256)S(1)} %get-tuple-element.64, f32[1536]{0:T(1024)S(1)} %copy-done.70), channel_id=1, replica_groups=mesh['seq'=16,'tp'=2] {'seq'}, use_global_device_ids=true, to_apply=%region_35.36 | all-reduce | flops 2112 | bytes 16896 | tf_op jit(solution)/shard_map/psum | solution.py:289
  1036.5 2.9 fusion.36
  1039.5 39.5 %all-reduce = (f32[768]{0:T(1024)}, f32[768]{0:T(1024)}, f32[768]{0:T(1024)}, f32[768]{0:T(1024)}, f32[768]{0:T(1024)}, /*index=5*/f32[768]{0:T(1024)}) all-reduce(f32[768]{0:T(1024)S(1)} %get-tuple-element.20, f32[768]{0:T(1024)S(1)} %get-tuple-element.25, f32[768]{0:T(1024)S(1)} %copy-done.68, ...), channel_id=1, replica_groups=mesh['seq'=16,'tp'=2] {'seq','tp'}, use_global_device_ids=true, to_apply=%region_30.31 | all-reduce | flops 4608 | bytes 36864 | tf_op jit(solution)/shard_map/psum | solution.py:310
  1079.0 4.1 fusion.28
  1083.1 158.4 %all-reduce.5.cloned.1.call-done = (f32[768,384]{1,0:T(8,128)}, f32[768,384]{1,0:T(8,128)}, f32[768,192]{0,1:T(8,128)}, f32[384,768]{1,0:T(8,128)}, f32[768,1536]{1,0:T(8,128)}, /*index=5*/f32[1536,768]{1,0:T(8,128)}) async-done(((f32[768,384]{1,0:T(8,128)}, f32[768,384]{1,0:T(8,128)}, f32[768,192]{0,1:T(8,128)}, f32[384,768]{1,0:T(8,128)}, f32[768,1536]{1,0:T(8,128)}, /*index=5*/f32[1536,768]{1,0:T(8,128)}), ...) | async-done | bytes 13565968 | tf_op jit(solution)/shard_map/psum | solution.py:289
  (305 shorter events, 85.0 us)
Async XLA Ops:
  7.2 384.6 %copy-start = (bf16[768,1536]{1,0:T(8,128)(2,1)S(1)}, bf16[768,1536]{1,0:T(8,128)(2,1)}, u32[]{:S(2)}) copy-start(bf16[768,1536]{1,0:T(8,128)(2,1)} %param.35) | copy-start | bytes 7077892
  7.2 54.2 %all-gather.5.cloned.1.call-start = ((), (), s32[]{:S(2)}) async-start(), calls=%async_computation.4 | async-start | bytes 4718592 | tf_op jit(solution)/shard_map/all_gather | solution.py:126
  9.1 52.3 %copy-start.55 = (bf16[768,192]{0,1:T(8,128)(2,1)S(1)}, bf16[768,192]{0,1:T(8,128)(2,1)}, u32[]{:S(2)}) copy-start(bf16[768,192]{0,1:T(8,128)(2,1)} %param.29) | copy-start | bytes 884740
  9.2 52.3 %copy-start.82 = (f32[192]{0:T(256)S(1)}, f32[192]{0:T(256)}, u32[]{:S(2)}) copy-start(f32[192]{0:T(256)} %param.30) | copy-start | bytes 2308
  13.7 50.9 %copy-start.50 = (bf16[2048,192]{0,1:T(8,128)(2,1)S(1)}, bf16[2048,192]{0,1:T(8,128)(2,1)}, u32[]{:S(2)}) copy-start(bf16[2048,192]{0,1:T(8,128)(2,1)} %param.21) | copy-start | bytes 2359300
  13.7 327.2 %reduce-scatter.5.cloned.1.call-start = ((), (), s32[]{:S(2)}) async-start(), calls=%async_computation.5 | async-start | bytes 4718592 | tf_op jit(solution)/shard_map/reduce_scatter | solution.py:178
  69.7 10.9 copy-start.74
  69.7 11.0 copy-start.62
  69.7 5.7 collective-permute-start
  79.1 8.3 copy-start.81
  79.1 137.9 %collective-permute-start.1 = (bf16[2,2,2048,384]{2,3,1,0:T(8,128)(2,1)}, bf16[2,2,2048,384]{2,3,1,0:T(8,128)(2,1)}, u32[]{:S(2)}, u32[]{:S(2)}) collective-permute-start(bf16[2,2,2048,384]{2,3,1,0:T(8,128)(2,1)} %pad_maximum_fusion), channel_id=1, source_target_pairs={{0,4},{4,0},{2,6},{6,2},{8,12},{12,8},{10,14},{14,10},{16,20},{20,... | collective-permute-start | bytes 18874376 | tf_op jit(solution)/shard_map/ppermute | solution.py:21
  80.7 6.7 copy-start.42
  96.0 134.4 %copy-start.8 = (bf16[48,8,8,256]{3,2,1,0:T(8,128)(2,1)}, bf16[48,8,8,256]{3,2,1,0:T(8,128)(2,1)S(1)}, u32[]{:S(2)}) copy-start(bf16[48,8,8,256]{3,2,1,0:T(8,128)(2,1)S(1)} %copy.217) | copy-start | bytes 4718596
  96.5 176.1 %copy-start.20 = (bf16[48,8,8,256]{3,2,1,0:T(8,128)(2,1)}, bf16[48,8,8,256]{3,2,1,0:T(8,128)(2,1)S(1)}, u32[]{:S(2)}) copy-start(bf16[48,8,8,256]{3,2,1,0:T(8,128)(2,1)S(1)} %copy.216) | copy-start | bytes 4718596
  103.3 160.1 %copy-start.28 = (bf16[48,8,8,256]{3,2,1,0:T(8,128)(2,1)}, bf16[48,8,8,256]{3,2,1,0:T(8,128)(2,1)S(1)}, u32[]{:S(2)}) copy-start(bf16[48,8,8,256]{3,2,1,0:T(8,128)(2,1)S(1)} %copy.222) | copy-start | bytes 4718596
  222.6 31.5 %copy-start.22 = (bf16[48,8,8,256]{3,2,1,0:T(8,128)(2,1)}, bf16[48,8,8,256]{3,2,1,0:T(8,128)(2,1)S(1)}, u32[]{:S(2)}) copy-start(bf16[48,8,8,256]{3,2,1,0:T(8,128)(2,1)S(1)} %copy.223) | copy-start | bytes 4718596
  223.1 7.4 copy-start.18
  223.6 6.8 copy-start.38
  233.4 48.5 %copy-start.2 = (f32[8,6,256,256]{2,3,1,0:T(8,128)}, f32[8,6,256,256]{2,3,1,0:T(8,128)S(1)}, u32[]{:S(2)}) copy-start(f32[8,6,256,256]{2,3,1,0:T(8,128)S(1)} %get-tuple-element.80) | copy-start | bytes 37748740
  297.4 43.5 %copy-start.59 = (f32[768]{0:T(1024)S(1)}, f32[768]{0:T(1024)}, u32[]{:S(2)}) copy-start(f32[768]{0:T(1024)} %param.32) | copy-start | bytes 9220
  297.4 47.2 %copy-start.65 = (f32[768]{0:T(1024)S(1)}, f32[768]{0:T(1024)}, u32[]{:S(2)}) copy-start(f32[768]{0:T(1024)} %param.33) | copy-start | bytes 9220
  297.4 47.2 %copy-start.73 = (f32[768]{0:T(1024)S(1)}, f32[768]{0:T(1024)}, u32[]{:S(2)}) copy-start(f32[768]{0:T(1024)} %param.34) | copy-start | bytes 9220
  297.4 94.4 %all-gather.7.cloned.1.call-start = ((), (), s32[]{:S(2)}) async-start(), calls=%async_computation.6 | async-start | bytes 4718592 | tf_op jit(solution)/shard_map/all_gather | solution.py:187
  344.6 47.2 %copy-start.80 = (f32[1536]{0:T(1024)S(1)}, f32[1536]{0:T(1024)}, u32[]{:S(2)}) copy-start(f32[1536]{0:T(1024)} %param.36) | copy-start | bytes 18436
  346.7 91.5 %all-gather.9.cloned.1.call-start = ((), (), s32[]{:S(2)}) async-start(), calls=%async_computation.8 | async-start | bytes 4718592 | tf_op jit(solution)/shard_map/all_gather | solution.py:200
  347.3 161.0 %reduce-scatter.9.cloned.1.call-start = ((), (), s32[]{:S(2)}) async-start(), calls=%async_computation.9 | async-start | bytes 4718592 | tf_op jit(solution)/shard_map/reduce_scatter | solution.py:206
  464.8 89.6 %reduce-scatter.7.cloned.1.call-start = ((), (), s32[]{:S(2)}) async-start(), calls=%async_computation.7 | async-start | bytes 4718592 | tf_op jit(solution)/shard_map/reduce_scatter | solution.py:191
  476.0 32.3 %copy-start.5 = (bf16[1024,768]{1,0:T(8,128)(2,1)S(1)}, bf16[1024,768]{1,0:T(8,128)(2,1)}, u32[]{:S(2)}) copy-start(bf16[1024,768]{1,0:T(8,128)(2,1)} %param.20) | copy-start | bytes 4718596
  476.0 78.3 %copy-start.72 = (f32[768]{0:T(1024)S(1)}, f32[768]{0:T(1024)}, u32[]{:S(2)}) copy-start(f32[768]{0:T(1024)} %param.38) | copy-start | bytes 9220
  476.0 132.0 %all-gather.11.cloned.1.call-start = ((), (), s32[]{:S(2)}) async-start(), calls=%async_computation.10 | async-start | bytes 4718592 | tf_op jit(solution)/shard_map/all_gather | solution.py:216
  561.6 46.4 %copy-start.79 = (bf16[384,768]{1,0:T(8,128)(2,1)S(1)}, bf16[384,768]{1,0:T(8,128)(2,1)}, u32[]{:S(2)}) copy-start(bf16[384,768]{1,0:T(8,128)(2,1)} %param.31) | copy-start | bytes 1769476
  562.9 473.6 %reduce-scatter.11.cloned.1.call-start = ((), (), s32[]{:S(2)}) async-start(), calls=%async_computation.11 | async-start | bytes 4718592 | tf_op jit(solution)/shard_map/reduce_scatter | solution.py:273
  624.2 9.0 copy-start.23
  639.6 6.4 copy-start.21
  646.0 6.6 copy-start.25
  689.2 42.7 %copy-start.9 = (bf16[48,8,8,256]{3,2,1,0:T(8,128)(2,1)S(1)}, bf16[48,8,8,256]{3,2,1,0:T(8,128)(2,1)}, u32[]{:S(2)}) copy-start(bf16[48,8,8,256]{3,2,1,0:T(8,128)(2,1)} %copy-done.8) | copy-start | bytes 4718596
  742.8 14.6 %slice-start.3 = ((s8[12582912]{0:T(1024)(128)(4,1)}), s8[4194304]{0:T(1024)(128)(4,1)S(1)}, s32[]{:S(2)}) async-start(s8[12582912]{0:T(1024)(128)(4,1)} %bitcast.177), calls=%async_computation.16 | async-start | bytes 8388608
  742.8 14.6 %slice-start.4 = ((s8[12582912]{0:T(1024)(128)(4,1)}), s8[4194304]{0:T(1024)(128)(4,1)S(1)}, s32[]{:S(2)}) async-start(s8[12582912]{0:T(1024)(128)(4,1)} %bitcast.177), calls=%async_computation.17 | async-start | bytes 8388608
  749.3 137.6 %collective-permute-start.2 = (bf16[2,2,8,256,6,64]{3,5,4,2,1,0:T(8,128)(2,1)}, bf16[2,2,8,256,6,64]{3,5,4,2,1,0:T(8,128)(2,1)}, u32[]{:S(2)}, u32[]{:S(2)}) collective-permute-start(bf16[2,2,8,256,6,64]{3,5,4,2,1,0:T(8,128)(2,1)} %pad_maximum_fusion.1), channel_id=1, source_target_pairs={{0,4},{4,0},{2,6},{6,2},{8,12},{12,8},{10,14},{14,10},{16,20},{20,... | collective-permute-start | bytes 18874376 | tf_op jit(solution)/shard_map/ppermute | solution.py:21
  750.8 6.6 slice-start.5
  761.9 13.1 %slice-start = ((s8[12582912]{0:T(1024)(128)(4,1)}), s8[4194304]{0:T(1024)(128)(4,1)S(1)}, s32[]{:S(2)}) async-start(s8[12582912]{0:T(1024)(128)(4,1)} %bitcast.175), calls=%async_computation.13 | async-start | bytes 8388608
  761.9 13.1 %slice-start.1 = ((s8[12582912]{0:T(1024)(128)(4,1)}), s8[4194304]{0:T(1024)(128)(4,1)S(1)}, s32[]{:S(2)}) async-start(s8[12582912]{0:T(1024)(128)(4,1)} %bitcast.175), calls=%async_computation.14 | async-start | bytes 8388608
  768.4 6.6 slice-start.2
  779.5 123.8 %slice-start.8 = ((s8[6291456]{0:T(1024)(128)(4,1)}), s8[4194304]{0:T(1024)(128)(4,1)S(1)}, s32[]{:S(2)}) async-start(s8[6291456]{0:T(1024)(128)(4,1)} %bitcast.189), calls=%async_computation.21 | async-start | bytes 8388608
  779.5 124.9 %slice-start.12 = ((s8[6291456]{0:T(1024)(128)(4,1)}), s8[4194304]{0:T(1024)(128)(4,1)S(1)}, s32[]{:S(2)}) async-start(s8[6291456]{0:T(1024)(128)(4,1)} %bitcast.193), calls=%async_computation.25 | async-start | bytes 8388608
  782.4 120.9 %slice-start.9 = ((s8[6291456]{0:T(1024)(128)(4,1)}), s8[2097152]{0:T(1024)(128)(4,1)S(1)}, s32[]{:S(2)}) async-start(s8[6291456]{0:T(1024)(128)(4,1)} %bitcast.189), calls=%async_computation.22 | async-start | bytes 4194304
  782.4 122.0 %slice-start.13 = ((s8[6291456]{0:T(1024)(128)(4,1)}), s8[2097152]{0:T(1024)(128)(4,1)S(1)}, s32[]{:S(2)}) async-start(s8[6291456]{0:T(1024)(128)(4,1)} %bitcast.193), calls=%async_computation.26 | async-start | bytes 4194304
  898.2 7.6 slice-start.10
  903.3 15.1 %collective-permute-start.3 = (bf16[1,2,8,256,6,64]{3,5,4,2,1,0:T(8,128)(2,1)}, bf16[1,2,8,256,6,64]{3,5,4,2,1,0:T(8,128)(2,1)}, u32[]{:S(2)}, u32[]{:S(2)}) collective-permute-start(bf16[1,2,8,256,6,64]{3,5,4,2,1,0:T(8,128)(2,1)} %slice.79), channel_id=1, source_target_pairs={{0,2},{2,0},{4,6},{6,4},{8,10},{10,8},{12,14},{14,12},{16,18},{18,... | collective-permute-start | bytes 9437192 | tf_op jit(solution)/shard_map/ppermute | solution.py:21
  906.3 12.1 slice-start.14
  909.0 9.4 slice-start.15
  909.1 9.4 slice-start.16
  938.1 303.4 %all-reduce.5.cloned.1.call-start = ((), (), s32[]{:S(2)}) async-start(), calls=%async_computation.12 | async-start | bytes 27131904 | tf_op jit(solution)/shard_map/psum | solution.py:289
  938.2 10.0 copy-start.75
  948.1 8.9 copy-start.45
  948.1 8.9 copy-start.76
  969.0 67.5 %copy-start.6 = (bf16[1024,768]{1,0:T(8,128)(2,1)S(1)}, bf16[1024,768]{1,0:T(8,128)(2,1)}, u32[]{:S(2)}) copy-start(bf16[1024,768]{1,0:T(8,128)(2,1)} %param.20) | copy-start | bytes 4718596
  969.0 67.5 %copy-start.58 = (f32[1024]{0:T(1024)S(1)}, f32[1024]{0:T(1024)}, u32[]{:S(2)}) copy-start(f32[1024]{0:T(1024)} %copy-done.57) | copy-start | bytes 12292
  969.0 67.5 %copy-start.61 = (f32[1024]{0:T(1024)S(1)}, f32[1024]{0:T(1024)}, u32[]{:S(2)}) copy-start(f32[1024]{0:T(1024)} %copy-done.60) | copy-start | bytes 12292
  969.0 67.5 %copy-start.64 = (f32[768]{0:T(1024)S(1)}, f32[768]{0:T(1024)}, u32[]{:S(2)}) copy-start(f32[768]{0:T(1024)} %param.24) | copy-start | bytes 9220
  969.1 70.3 %copy-start.66 = (f32[768]{0:T(1024)S(1)}, f32[768]{0:T(1024)}, u32[]{:S(2)}) copy-start(f32[768]{0:T(1024)} %get-tuple-element.18) | copy-start | bytes 9220
  969.1 70.3 %copy-start.67 = (f32[768]{0:T(1024)S(1)}, f32[768]{0:T(1024)}, u32[]{:S(2)}) copy-start(f32[768]{0:T(1024)} %get-tuple-element.24) | copy-start | bytes 9220
  969.1 70.3 %copy-start.68 = (f32[768]{0:T(1024)S(1)}, f32[768]{0:T(1024)}, u32[]{:S(2)}) copy-start(f32[768]{0:T(1024)} %get-tuple-element.57) | copy-start | bytes 9220
  969.1 70.3 %copy-start.69 = (f32[768]{0:T(1024)S(1)}, f32[768]{0:T(1024)}, u32[]{:S(2)}) copy-start(f32[768]{0:T(1024)} %get-tuple-element.68) | copy-start | bytes 9220
  (53 other events, 155.6 us)
Sparse Core Ops, SparseCore 0:
  13.8 47.6 all-gather.4
  297.5 43.3 reduce-scatter.4
  346.8 44.9 all-gather.6
  393.3 44.9 all-gather.8
  464.9 43.3 reduce-scatter.8
  510.9 43.3 reduce-scatter.6
  563.0 44.9 all-gather.10
  938.2 43.3 reduce-scatter.10
  988.6 252.8 all-reduce.4
where the time goes:
time: 1260 us
  waiting for transfers between devices  664 us (53%)
  matrix products  269 us (21%)
  other arithmetic  145 us (12%)
  blocking collectives  104 us (8%)
  local copies, waits for them, and re-layouts  58.9 us (5%)
  between operations  15.3 us (1%)
    ppermute x4, waiting for transfers between devices, from_partner(): return lax.ppermute(block, axis, route)  217 us
    psum x1, waiting for transfers between devices, per_device(): lax.psum((grad_query_weight, grad_query_bias, grad_key_weight, grad_value...  158 us
    psum x1, blocking collectives, per_device(): lax.psum((grad_query_weight, grad_query_bias, grad_key_weight, grad_value...  64 us
    dot_general x4, matrix products, per_device(): jnp.einsum('bqhe,bkhe->bhqk', grad_heads, value_heads, preferred_element_...  56 us
    all_gather x1, waiting for transfers between devices, per_device(): lax.all_gather(first_norm.astype(jnp.bfloat16), 'tp', axis=0, tiled=True)  47.7 us
    all_gather x1, waiting for transfers between devices, per_device(): lax.all_gather(middle_grad.astype(jnp.bfloat16), 'tp', axis=0, tiled=True)  45 us
    all_gather x1, waiting for transfers between devices, per_device(): lax.all_gather(second_norm.astype(jnp.bfloat16), 'tp', axis=0, tiled=True)  44.5 us
    reduce_scatter x1, waiting for transfers between devices, per_device(): lax.psum_scatter(product(attended_rows, out_weight).astype(jnp.bfloat16),...  43.4 us
  transfers between devices with their start and end apart: 13, of which 11 were waited for; matrix products, arithmetic and copies ran while one was open for 11% of the time, Pallas kernels for 0%

commit v1 on v0

--- a/solution.py
+++ b/solution.py
@@ -9,6 +9,23 @@
 SEQ_LEN = 1024
 BLOCK = 256
 EPSILON = 1e-05
+
+
+def joined_along(pieces, dim):
+    shape = list(pieces.shape[1:])
+    shape[dim] *= pieces.shape[0]
+    return jnp.moveaxis(pieces, 0, dim).reshape(shape)
+
+
+def grow_blocks(x, axis):
+    devices, index = (lax.axis_size(axis), lax.axis_index(axis))
+    pieces, distance = (x[None], 1)
+    while distance < devices:
+        other = lax.ppermute(pieces, axis, [(i, i ^ distance) for i in range(devices)])
+        low = index & distance == 0
+        pieces = jnp.concatenate([jnp.where(low, pieces, other), jnp.where(low, other, pieces)])
+        distance *= 2
+    return pieces
 
 
 def from_partner(block, axis, apart):
@@ -197,7 +214,7 @@
     layer_out = (middle + feed_out + down_bias).astype(jnp.bfloat16)
     grad_output = out_grad.astype(jnp.float32)
     grad_down_bias = jnp.sum(grad_output, axis=0)
-    grad_rows_all = lax.all_gather(out_grad, "tp", axis=0, tiled=True)
+    grad_rows_all = joined_along(grow_blocks(out_grad, "tp"), 0)
     grad_down_weight = product_lt(activated_low, grad_rows_all)
     grad_hidden = gelu_back(product_rt(grad_rows_all, down_weight))[0]
     grad_up_bias = jnp.sum(grad_hidden, axis=0)

time: 1260 us -> 1250 us (level)
    ppermute x0 -> x1, waiting for transfers between devices: none -> 62.5 us  [grow_blocks(): lax.ppermute(pieces, axis, [(i, i ^ distance) for i in range(devices)])]
    all_gather x1, waiting for transfers between devices: 44.5 us -> 3.47 us  [per_device(): lax.all_gather(second_norm.astype(jnp.bfloat16), 'tp', axis=0, tiled=True)]
    all_gather x1 -> x0, waiting for transfers between devices: 33.1 us -> none  [per_device(): grad_rows_all = lax.all_gather(out_grad, 'tp', axis=0, tiled=True)]
    unnamed x226 -> x230, local copies, waits for them, and re-layouts: 35.7 us -> 35.8 us
where the time goes in v1:
time: 1250 us
  waiting for transfers between devices  652 us (52%)
  matrix products  267 us (21%)
  other arithmetic  149 us (12%)
  blocking collectives  104 us (8%)
  local copies, waits for them, and re-layouts  59.1 us (5%)
  between operations  15.4 us (1%)
    ppermute x4, waiting for transfers between devices, from_partner(): return lax.ppermute(block, axis, route)  217 us
    psum x1, waiting for transfers between devices, per_device(): lax.psum((grad_query_weight, grad_query_bias, grad_key_weight, grad_value...  157 us
    psum x1, blocking collectives, per_device(): lax.psum((grad_query_weight, grad_query_bias, grad_key_weight, grad_value...  64.2 us
    ppermute x1, waiting for transfers between devices, grow_blocks(): lax.ppermute(pieces, axis, [(i, i ^ distance) for i in range(devices)])  62.5 us
    dot_general x4, matrix products, per_device(): jnp.einsum('bqhe,bkhe->bhqk', grad_heads, value_heads, preferred_element_...  56.1 us
    all_gather x1, waiting for transfers between devices, per_device(): lax.all_gather(first_norm.astype(jnp.bfloat16), 'tp', axis=0, tiled=True)  47.7 us
    all_gather x1, waiting for transfers between devices, per_device(): lax.all_gather(middle_grad.astype(jnp.bfloat16), 'tp', axis=0, tiled=True)  45 us
    reduce_scatter x1, waiting for transfers between devices, per_device(): lax.psum_scatter(product(attended_rows, out_weight).astype(jnp.bfloat16),...  43.4 us
  transfers between devices with their start and end apart: 13, of which 11 were waited for; matrix products, arithmetic and copies ran while one was open for 11% of the time, Pallas kernels for 0%

profile of v1, /device:TPU:0, one launch (start us, length us, event | category | flops | bytes accessed | tf_op | source)
XLA Modules:
  0.0 1249.4 jit_solution(3745732338274830790)
XLA Ops:
  13.7 47.7 %all-gather.4.cloned.1.call-done = bf16[2048,768]{1,0:T(8,128)(2,1)} async-done(((bf16[1024,768]{1,0:T(8,128)(2,1)}), bf16[2048,768]{1,0:T(8,128)(2,1)}) %all-gather.4.cloned.1.call-update) | async-done | bytes 3145744 | tf_op jit(solution)/shard_map/all_gather | solution.py:143
  61.4 3.1 fusion.40
  69.7 5.7 collective-permute-done
  75.3 3.5 pad_maximum_fusion
  81.2 4.5 compare_and_fusion.2
  87.3 4.0 add_convert_fusion.4
  96.5 6.0 fusion.6
  103.8 6.0 fusion.7
  109.7 107.2 %collective-permute-done.1 = bf16[2,2,2048,384]{2,3,1,0:T(8,128)(2,1)} collective-permute-done((bf16[2,2,2048,384]{2,3,1,0:T(8,128)(2,1)}, bf16[2,2,2048,384]{2,3,1,0:T(8,128)(2,1)}, u32[]{:S(2)}, u32[]{:S(2)}) %collective-permute-start.1) | collective-permute-done | bytes 6291488 | tf_op jit(solution)/shard_map/ppermute | solution.py:38
  216.9 3.5 fusion.105
  224.0 6.2 fusion.8
  230.2 2.9 fusion.9
  233.2 20.6 %exponential_reduce_fusion.2 = (f32[8,6,256]{2,1,0:T(8,128)S(1)}, f32[8,6,256]{2,1,0:T(8,128)S(1)}, f32[8,6,256]{2,1,0:T(8,128)S(1)}, f32[8,6,256]{2,1,0:T(8,128)S(1)}) fusion(f32[8,6,256,256]{2,3,1,0:T(8,128)} %get-tuple-element.88, f32[8,6,256]{2,1,0:T(8,128)S(1)} %maximum_maximum_fusion, pred[8,256,256]{1,2,0:T(8,128)(4,1)S(1)} %copy-done.24, ...), kind=kLoop, calls=%fused_computation.24 | loop fusion | flops 50282496 | bytes 52674560 | tf_op jit(solution)/shard_map/reduce_sum | solution.py:177
  253.8 9.3 fusion.51
  263.1 9.3 fusion.55
  272.4 9.2 fusion.59
  281.6 8.2 fusion.45
  293.9 3.5 convolution_convert_fusion
  297.5 43.4 %reduce-scatter.5.cloned.1.call-done = bf16[1024,768]{1,0:T(8,128)(2,1)} async-done(((bf16[2048,768]{1,0:T(8,128)(2,1)}), bf16[1024,768]{1,0:T(8,128)(2,1)}) %reduce-scatter.5.cloned.1.call-update) | async-done | bytes 1572880 | tf_op jit(solution)/shard_map/reduce_scatter | solution.py:195
  341.0 2.6 fusion.76
  347.2 62.5 %collective-permute-done.2 = bf16[1,1024,768]{2,1,0:T(8,128)(2,1)} collective-permute-done((bf16[1,1024,768]{2,1,0:T(8,128)(2,1)}, bf16[1,1024,768]{2,1,0:T(8,128)(2,1)}, u32[]{:S(2)}, u32[]{:S(2)}) %collective-permute-start.2) | collective-permute-done | bytes 1572896 | tf_op jit(solution)/shard_map/ppermute | solution.py:24
  413.7 3.5 all-gather.6.cloned.1.call-done
  417.2 13.5 %multiply_convert_fusion.4 = (bf16[2048,1536]{1,0:T(8,128)(2,1)}, f32[2048,1536]{1,0:T(8,128)}) fusion(f32[1536]{0:T(1024)S(1)} %copy-done.82, bf16[2048,768]{1,0:T(8,128)(2,1)} %all-gather.6.cloned.1.call-done, bf16[768,1536]{1,0:T(8,128)(2,1)S(1)} %copy-done), kind=kOutput, calls=%fused_computation.17 | convolution fusion | flops 4863295488 | bytes 24385536 | tf_op jit(solution)/shard_map/dot_general | solution.py:42
  430.7 14.7 %fusion.107 = (f32[1536]{0:T(1024)}, bf16[2048,1536]{1,0:T(8,128)(2,1)S(1)}) fusion(f32[2048,1536]{1,0:T(8,128)} %get-tuple-element.90, f32[1536]{0:T(1024)S(1)} %copy-done.82, bf16[2048,768]{1,0:T(8,128)(2,1)S(1)} %bitcast.251, bf16[1536,768]{1,0:T(8,128)(2,1)S(1)} %copy-done.78), kind=kOutput, calls=%fused_computation.202 | convolution fusion | flops 4901042688 | bytes 24391680 | tf_op jit(solution)/shard_map/dot_general | solution.py:46
  448.1 6.4 convolution_convert_fusion.1
  456.1 9.2 convolution_convert_fusion.2
  465.4 32.6 %reduce-scatter.9.cloned.1.call-done = bf16[1024,768]{1,0:T(8,128)(2,1)} async-done(((bf16[2048,768]{1,0:T(8,128)(2,1)}), bf16[1024,768]{1,0:T(8,128)(2,1)}) %reduce-scatter.9.cloned.1.call-update) | async-done | bytes 1572880 | tf_op jit(solution)/shard_map/reduce_scatter | solution.py:223
  498.0 4.1 fusion.35
  502.1 42.0 %reduce-scatter.7.cloned.1.call-done = bf16[1024,768]{1,0:T(8,128)(2,1)} async-done(((bf16[2048,768]{1,0:T(8,128)(2,1)}), bf16[1024,768]{1,0:T(8,128)(2,1)}) %reduce-scatter.7.cloned.1.call-update) | async-done | bytes 1572880 | tf_op jit(solution)/shard_map/reduce_scatter | solution.py:208
  544.0 5.6 fusion.104
  552.8 45.0 %all-gather.8.cloned.1.call-done = bf16[2048,768]{1,0:T(8,128)(2,1)} async-done(((bf16[1024,768]{1,0:T(8,128)(2,1)}), bf16[2048,768]{1,0:T(8,128)(2,1)}) %all-gather.8.cloned.1.call-update) | async-done | bytes 3145744 | tf_op jit(solution)/shard_map/all_gather | solution.py:233
  597.8 3.7 convolution_convert_fusion.3
  605.3 8.9 fusion.41
  614.2 9.0 fusion.42
  623.2 6.4 fusion.49
  629.6 6.4 fusion.46
  636.0 6.8 fusion.57
  642.8 36.5 %multiply_reduce_fusion.2 = (f32[8,6,256]{2,1,0:T(8,128)S(1)}, f32[8,6,256]{2,1,0:T(8,128)S(1)}, f32[8,6,256]{2,1,0:T(8,128)S(1)}, f32[8,6,256]{2,1,0:T(8,128)S(1)}, f32[8,6,256,256]{2,3,1,0:T(8,128)}) fusion(f32[8,6,256,256]{2,3,1,0:T(8,128)} %get-tuple-element.88, f32[8,6,256]{2,1,0:T(8,128)S(1)} %log_add_fusion, pred[8,256,256]{1,2,0:T(8,128)(4,1)S(1)} %copy-done.25, ...), kind=kOutput, calls=%fused_computation.15 | convolution fusion | flops 465518592 | bytes 106151936 | tf_op jit(solution)/shard_map/bqhe,bkhe->bhqk/dot_general | solution.py:241
  679.4 42.5 %multiply_convert_fusion.1 = (bf16[8,6,256,256]{2,3,1,0:T(8,128)(2,1)}, bf16[8,6,256,256]{2,3,1,0:T(8,128)(2,1)}, bf16[8,6,256,256]{2,3,1,0:T(8,128)(2,1)}, bf16[8,6,256,256]{2,3,1,0:T(8,128)(2,1)}) fusion(f32[8,6,256,256]{2,3,1,0:T(8,128)} %fusion.49, f32[8,6,256,256]{2,3,1,0:T(8,128)} %get-tuple-element.84, f32[8,6,256]{2,1,0:T(8,128)S(1)} %add_add_fusion, ...), kind=kLoop, calls=%fused_computation.10 | loop fusion | flops 75497472 | bytes 128024576 | tf_op jit(solution)/shard_map/convert_element_type | solution.py:251
  721.9 5.0 fusion.43
  732.8 6.5 pad_maximum_fusion.1
  740.8 6.6 multiply_bitcast_fusion
  747.5 4.5 convolution_bitcast_fusion
  751.9 6.5 maximum_bitcast_fusion.1
  758.4 6.6 multiply_bitcast_fusion.1
  765.1 4.5 convolution_bitcast_fusion.1
  769.5 2.8 maximum_bitcast_fusion
  772.4 104.5 %collective-permute-done.3 = bf16[2,2,8,256,6,64]{3,5,4,2,1,0:T(8,128)(2,1)} collective-permute-done((bf16[2,2,8,256,6,64]{3,5,4,2,1,0:T(8,128)(2,1)}, bf16[2,2,8,256,6,64]{3,5,4,2,1,0:T(8,128)(2,1)}, u32[]{:S(2)}, u32[]{:S(2)}) %collective-permute-start.3) | collective-permute-done | bytes 6291488 | tf_op jit(solution)/shard_map/ppermute | solution.py:38
  876.9 11.5 maximum_add_fusion
  888.4 5.1 slice.79
  896.5 2.7 fusion.72
  899.3 6.0 bitcast_convert_fusion
  908.6 5.7 slice_add_fusion
  924.6 3.7 add_convert_fusion
  928.3 9.9 fusion.112
  938.3 9.7 fusion.37
  950.4 2.9 fusion.109
  954.9 2.9 fusion.110
  960.0 3.3 slice_reduce_fusion
  963.4 64.2 %all-reduce.1 = (f32[384]{0:T(512)}, f32[192]{0:T(256)}, f32[1536]{0:T(1024)}) all-reduce(f32[384]{0:T(512)S(1)} %reduce_sum.290, f32[192]{0:T(256)S(1)} %get-tuple-element.64, f32[1536]{0:T(1024)S(1)} %copy-done.71), channel_id=1, replica_groups=mesh['seq'=16,'tp'=2] {'seq'}, use_global_device_ids=true, to_apply=%region_35.36 | all-reduce | flops 2112 | bytes 16896 | tf_op jit(solution)/shard_map/psum | solution.py:306
  1027.6 3.0 fusion.36
  1030.6 39.5 %all-reduce = (f32[768]{0:T(1024)}, f32[768]{0:T(1024)}, f32[768]{0:T(1024)}, f32[768]{0:T(1024)}, f32[768]{0:T(1024)}, /*index=5*/f32[768]{0:T(1024)}) all-reduce(f32[768]{0:T(1024)S(1)} %get-tuple-element.20, f32[768]{0:T(1024)S(1)} %get-tuple-element.25, f32[768]{0:T(1024)S(1)} %copy-done.69, ...), channel_id=1, replica_groups=mesh['seq'=16,'tp'=2] {'seq','tp'}, use_global_device_ids=true, to_apply=%region_30.31 | all-reduce | flops 4608 | bytes 36864 | tf_op jit(solution)/shard_map/psum | solution.py:327
  1070.2 4.1 fusion.28
  1074.3 157.4 %all-reduce.5.cloned.1.call-done = (f32[768,384]{1,0:T(8,128)}, f32[768,384]{1,0:T(8,128)}, f32[768,192]{0,1:T(8,128)}, f32[384,768]{1,0:T(8,128)}, f32[768,1536]{1,0:T(8,128)}, /*index=5*/f32[1536,768]{1,0:T(8,128)}) async-done(((f32[768,384]{1,0:T(8,128)}, f32[768,384]{1,0:T(8,128)}, f32[768,192]{0,1:T(8,128)}, f32[384,768]{1,0:T(8,128)}, f32[768,1536]{1,0:T(8,128)}, /*index=5*/f32[1536,768]{1,0:T(8,128)}), ...) | async-done | bytes 13565968 | tf_op jit(solution)/shard_map/psum | solution.py:306
  (310 shorter events, 89.2 us)
Async XLA Ops:
  7.2 410.0 %copy-start = (bf16[768,1536]{1,0:T(8,128)(2,1)S(1)}, bf16[768,1536]{1,0:T(8,128)(2,1)}, u32[]{:S(2)}) copy-start(bf16[768,1536]{1,0:T(8,128)(2,1)} %param.35) | copy-start | bytes 7077892
  7.2 54.2 %all-gather.4.cloned.1.call-start = ((), (), s32[]{:S(2)}) async-start(), calls=%async_computation.4 | async-start | bytes 4718592 | tf_op jit(solution)/shard_map/all_gather | solution.py:143
  9.1 52.3 %copy-start.56 = (bf16[768,192]{0,1:T(8,128)(2,1)S(1)}, bf16[768,192]{0,1:T(8,128)(2,1)}, u32[]{:S(2)}) copy-start(bf16[768,192]{0,1:T(8,128)(2,1)} %param.29) | copy-start | bytes 884740
  9.2 52.3 %copy-start.84 = (f32[192]{0:T(256)S(1)}, f32[192]{0:T(256)}, u32[]{:S(2)}) copy-start(f32[192]{0:T(256)} %param.30) | copy-start | bytes 2308
  13.7 50.9 %copy-start.51 = (bf16[2048,192]{0,1:T(8,128)(2,1)S(1)}, bf16[2048,192]{0,1:T(8,128)(2,1)}, u32[]{:S(2)}) copy-start(bf16[2048,192]{0,1:T(8,128)(2,1)} %param.21) | copy-start | bytes 2359300
  13.7 327.3 %reduce-scatter.5.cloned.1.call-start = ((), (), s32[]{:S(2)}) async-start(), calls=%async_computation.5 | async-start | bytes 4718592 | tf_op jit(solution)/shard_map/reduce_scatter | solution.py:195
  69.7 10.9 copy-start.75
  69.7 11.0 copy-start.63
  69.7 5.7 collective-permute-start
  79.1 8.2 copy-start.83
  79.1 137.9 %collective-permute-start.1 = (bf16[2,2,2048,384]{2,3,1,0:T(8,128)(2,1)}, bf16[2,2,2048,384]{2,3,1,0:T(8,128)(2,1)}, u32[]{:S(2)}, u32[]{:S(2)}) collective-permute-start(bf16[2,2,2048,384]{2,3,1,0:T(8,128)(2,1)} %pad_maximum_fusion), channel_id=1, source_target_pairs={{0,4},{4,0},{2,6},{6,2},{8,12},{12,8},{10,14},{14,10},{16,20},{20,... | collective-permute-start | bytes 18874376 | tf_op jit(solution)/shard_map/ppermute | solution.py:38
  80.7 6.6 copy-start.43
  96.0 134.2 %copy-start.8 = (bf16[48,8,8,256]{3,2,1,0:T(8,128)(2,1)}, bf16[48,8,8,256]{3,2,1,0:T(8,128)(2,1)S(1)}, u32[]{:S(2)}) copy-start(bf16[48,8,8,256]{3,2,1,0:T(8,128)(2,1)S(1)} %copy.217) | copy-start | bytes 4718596
  96.5 175.9 %copy-start.20 = (bf16[48,8,8,256]{3,2,1,0:T(8,128)(2,1)}, bf16[48,8,8,256]{3,2,1,0:T(8,128)(2,1)S(1)}, u32[]{:S(2)}) copy-start(bf16[48,8,8,256]{3,2,1,0:T(8,128)(2,1)S(1)} %copy.216) | copy-start | bytes 4718596
  103.2 159.9 %copy-start.28 = (bf16[48,8,8,256]{3,2,1,0:T(8,128)(2,1)}, bf16[48,8,8,256]{3,2,1,0:T(8,128)(2,1)S(1)}, u32[]{:S(2)}) copy-start(bf16[48,8,8,256]{3,2,1,0:T(8,128)(2,1)S(1)} %copy.222) | copy-start | bytes 4718596
  222.6 31.3 %copy-start.22 = (bf16[48,8,8,256]{3,2,1,0:T(8,128)(2,1)}, bf16[48,8,8,256]{3,2,1,0:T(8,128)(2,1)S(1)}, u32[]{:S(2)}) copy-start(bf16[48,8,8,256]{3,2,1,0:T(8,128)(2,1)S(1)} %copy.223) | copy-start | bytes 4718596
  223.1 7.1 copy-start.18
  223.6 6.6 copy-start.38
  233.2 48.5 %copy-start.2 = (f32[8,6,256,256]{2,3,1,0:T(8,128)}, f32[8,6,256,256]{2,3,1,0:T(8,128)S(1)}, u32[]{:S(2)}) copy-start(f32[8,6,256,256]{2,3,1,0:T(8,128)S(1)} %get-tuple-element.82) | copy-start | bytes 37748740
  297.4 43.5 %copy-start.60 = (f32[768]{0:T(1024)S(1)}, f32[768]{0:T(1024)}, u32[]{:S(2)}) copy-start(f32[768]{0:T(1024)} %param.32) | copy-start | bytes 9220
  297.5 47.2 %copy-start.66 = (f32[768]{0:T(1024)S(1)}, f32[768]{0:T(1024)}, u32[]{:S(2)}) copy-start(f32[768]{0:T(1024)} %param.33) | copy-start | bytes 9220
  297.5 47.2 %copy-start.74 = (f32[768]{0:T(1024)S(1)}, f32[768]{0:T(1024)}, u32[]{:S(2)}) copy-start(f32[768]{0:T(1024)} %param.34) | copy-start | bytes 9220
  297.5 119.7 %all-gather.6.cloned.1.call-start = ((), (), s32[]{:S(2)}) async-start(), calls=%async_computation.6 | async-start | bytes 4718592 | tf_op jit(solution)/shard_map/all_gather | solution.py:204
  346.8 151.2 %reduce-scatter.9.cloned.1.call-start = ((), (), s32[]{:S(2)}) async-start(), calls=%async_computation.8 | async-start | bytes 4718592 | tf_op jit(solution)/shard_map/reduce_scatter | solution.py:223
  346.8 62.9 %collective-permute-start.2 = (bf16[1,1024,768]{2,1,0:T(8,128)(2,1)}, bf16[1,1024,768]{2,1,0:T(8,128)(2,1)}, u32[]{:S(2)}, u32[]{:S(2)}) collective-permute-start(bf16[1,1024,768]{2,1,0:T(8,128)(2,1)} %bitcast.247), channel_id=1, source_target_pairs={{0,1},{1,0},{2,3},{3,2},{4,5},{5,4},{6,7},{7,6},{8,9},{9,8},{10,11... | collective-permute-start | bytes 4718600 | tf_op jit(solution)/shard_map/ppermute | solution.py:24
  417.2 13.6 %copy-start.41 = (bf16[2,1024,768]{2,1,0:T(8,128)(2,1)S(1)}, bf16[2,1024,768]{2,1,0:T(8,128)(2,1)}, u32[]{:S(2)}) copy-start(bf16[2,1024,768]{2,1,0:T(8,128)(2,1)} %pad_maximum_fusion.2) | copy-start | bytes 9437188
  417.2 13.6 %copy-start.78 = (bf16[1536,768]{1,0:T(8,128)(2,1)S(1)}, bf16[1536,768]{1,0:T(8,128)(2,1)}, u32[]{:S(2)}) copy-start(bf16[1536,768]{1,0:T(8,128)(2,1)} %param.37) | copy-start | bytes 7077892
  454.5 89.5 %reduce-scatter.7.cloned.1.call-start = ((), (), s32[]{:S(2)}) async-start(), calls=%async_computation.7 | async-start | bytes 4718592 | tf_op jit(solution)/shard_map/reduce_scatter | solution.py:208
  465.3 32.7 %copy-start.5 = (bf16[1024,768]{1,0:T(8,128)(2,1)S(1)}, bf16[1024,768]{1,0:T(8,128)(2,1)}, u32[]{:S(2)}) copy-start(bf16[1024,768]{1,0:T(8,128)(2,1)} %param.20) | copy-start | bytes 4718596
  465.3 78.7 %copy-start.73 = (f32[768]{0:T(1024)S(1)}, f32[768]{0:T(1024)}, u32[]{:S(2)}) copy-start(f32[768]{0:T(1024)} %param.38) | copy-start | bytes 9220
  465.4 132.5 %all-gather.8.cloned.1.call-start = ((), (), s32[]{:S(2)}) async-start(), calls=%async_computation.9 | async-start | bytes 4718592 | tf_op jit(solution)/shard_map/all_gather | solution.py:233
  551.4 46.4 %copy-start.81 = (bf16[384,768]{1,0:T(8,128)(2,1)S(1)}, bf16[384,768]{1,0:T(8,128)(2,1)}, u32[]{:S(2)}) copy-start(bf16[384,768]{1,0:T(8,128)(2,1)} %param.31) | copy-start | bytes 1769476
  552.7 474.8 %reduce-scatter.11.cloned.1.call-start = ((), (), s32[]{:S(2)}) async-start(), calls=%async_computation.10 | async-start | bytes 4718592 | tf_op jit(solution)/shard_map/reduce_scatter | solution.py:290
  614.2 9.0 copy-start.23
  636.0 6.8 copy-start.25
  679.4 42.5 %copy-start.9 = (bf16[48,8,8,256]{3,2,1,0:T(8,128)(2,1)S(1)}, bf16[48,8,8,256]{3,2,1,0:T(8,128)(2,1)}, u32[]{:S(2)}) copy-start(bf16[48,8,8,256]{3,2,1,0:T(8,128)(2,1)} %copy-done.8) | copy-start | bytes 4718596
  732.8 14.6 %slice-start.3 = ((s8[12582912]{0:T(1024)(128)(4,1)}), s8[4194304]{0:T(1024)(128)(4,1)S(1)}, s32[]{:S(2)}) async-start(s8[12582912]{0:T(1024)(128)(4,1)} %bitcast.181), calls=%async_computation.15 | async-start | bytes 8388608
  732.8 14.6 %slice-start.4 = ((s8[12582912]{0:T(1024)(128)(4,1)}), s8[4194304]{0:T(1024)(128)(4,1)S(1)}, s32[]{:S(2)}) async-start(s8[12582912]{0:T(1024)(128)(4,1)} %bitcast.181), calls=%async_computation.16 | async-start | bytes 8388608
  739.3 137.6 %collective-permute-start.3 = (bf16[2,2,8,256,6,64]{3,5,4,2,1,0:T(8,128)(2,1)}, bf16[2,2,8,256,6,64]{3,5,4,2,1,0:T(8,128)(2,1)}, u32[]{:S(2)}, u32[]{:S(2)}) collective-permute-start(bf16[2,2,8,256,6,64]{3,5,4,2,1,0:T(8,128)(2,1)} %pad_maximum_fusion.1), channel_id=1, source_target_pairs={{0,4},{4,0},{2,6},{6,2},{8,12},{12,8},{10,14},{14,10},{16,20},{20,... | collective-permute-start | bytes 18874376 | tf_op jit(solution)/shard_map/ppermute | solution.py:38
  740.8 6.6 slice-start.5
  751.9 13.1 %slice-start = ((s8[12582912]{0:T(1024)(128)(4,1)}), s8[4194304]{0:T(1024)(128)(4,1)S(1)}, s32[]{:S(2)}) async-start(s8[12582912]{0:T(1024)(128)(4,1)} %bitcast.179), calls=%async_computation.12 | async-start | bytes 8388608
  751.9 13.1 %slice-start.1 = ((s8[12582912]{0:T(1024)(128)(4,1)}), s8[4194304]{0:T(1024)(128)(4,1)S(1)}, s32[]{:S(2)}) async-start(s8[12582912]{0:T(1024)(128)(4,1)} %bitcast.179), calls=%async_computation.13 | async-start | bytes 8388608
  758.4 6.6 slice-start.2
  769.5 124.0 %slice-start.8 = ((s8[6291456]{0:T(1024)(128)(4,1)}), s8[4194304]{0:T(1024)(128)(4,1)S(1)}, s32[]{:S(2)}) async-start(s8[6291456]{0:T(1024)(128)(4,1)} %bitcast.193), calls=%async_computation.20 | async-start | bytes 8388608
  769.5 125.1 %slice-start.12 = ((s8[6291456]{0:T(1024)(128)(4,1)}), s8[4194304]{0:T(1024)(128)(4,1)S(1)}, s32[]{:S(2)}) async-start(s8[6291456]{0:T(1024)(128)(4,1)} %bitcast.197), calls=%async_computation.24 | async-start | bytes 8388608
  772.4 121.1 %slice-start.9 = ((s8[6291456]{0:T(1024)(128)(4,1)}), s8[2097152]{0:T(1024)(128)(4,1)S(1)}, s32[]{:S(2)}) async-start(s8[6291456]{0:T(1024)(128)(4,1)} %bitcast.193), calls=%async_computation.21 | async-start | bytes 4194304
  772.4 122.2 %slice-start.13 = ((s8[6291456]{0:T(1024)(128)(4,1)}), s8[2097152]{0:T(1024)(128)(4,1)S(1)}, s32[]{:S(2)}) async-start(s8[6291456]{0:T(1024)(128)(4,1)} %bitcast.197), calls=%async_computation.25 | async-start | bytes 4194304
  888.4 7.6 slice-start.10
  893.5 15.1 %collective-permute-start.4 = (bf16[1,2,8,256,6,64]{3,5,4,2,1,0:T(8,128)(2,1)}, bf16[1,2,8,256,6,64]{3,5,4,2,1,0:T(8,128)(2,1)}, u32[]{:S(2)}, u32[]{:S(2)}) collective-permute-start(bf16[1,2,8,256,6,64]{3,5,4,2,1,0:T(8,128)(2,1)} %slice.79), channel_id=1, source_target_pairs={{0,2},{2,0},{4,6},{6,4},{8,10},{10,8},{12,14},{14,12},{16,18},{18,... | collective-permute-start | bytes 9437192 | tf_op jit(solution)/shard_map/ppermute | solution.py:38
  896.5 12.1 slice-start.14
  899.2 9.4 slice-start.15
  899.2 9.4 slice-start.16
  928.3 303.4 %all-reduce.5.cloned.1.call-start = ((), (), s32[]{:S(2)}) async-start(), calls=%async_computation.11 | async-start | bytes 27131904 | tf_op jit(solution)/shard_map/psum | solution.py:306
  928.3 9.9 copy-start.76
  938.3 9.7 copy-start.46
  938.3 9.7 copy-start.77
  959.9 67.7 %copy-start.6 = (bf16[1024,768]{1,0:T(8,128)(2,1)S(1)}, bf16[1024,768]{1,0:T(8,128)(2,1)}, u32[]{:S(2)}) copy-start(bf16[1024,768]{1,0:T(8,128)(2,1)} %param.20) | copy-start | bytes 4718596
  959.9 67.7 %copy-start.59 = (f32[1024]{0:T(1024)S(1)}, f32[1024]{0:T(1024)}, u32[]{:S(2)}) copy-start(f32[1024]{0:T(1024)} %copy-done.58) | copy-start | bytes 12292
  959.9 67.7 %copy-start.62 = (f32[1024]{0:T(1024)S(1)}, f32[1024]{0:T(1024)}, u32[]{:S(2)}) copy-start(f32[1024]{0:T(1024)} %copy-done.61) | copy-start | bytes 12292
  959.9 67.7 %copy-start.65 = (f32[768]{0:T(1024)S(1)}, f32[768]{0:T(1024)}, u32[]{:S(2)}) copy-start(f32[768]{0:T(1024)} %param.24) | copy-start | bytes 9220
  960.0 70.6 %copy-start.67 = (f32[768]{0:T(1024)S(1)}, f32[768]{0:T(1024)}, u32[]{:S(2)}) copy-start(f32[768]{0:T(1024)} %get-tuple-element.18) | copy-start | bytes 9220
  960.0 70.6 %copy-start.68 = (f32[768]{0:T(1024)S(1)}, f32[768]{0:T(1024)}, u32[]{:S(2)}) copy-start(f32[768]{0:T(1024)} %get-tuple-element.24) | copy-start | bytes 9220
  960.0 70.6 %copy-start.69 = (f32[768]{0:T(1024)S(1)}, f32[768]{0:T(1024)}, u32[]{:S(2)}) copy-start(f32[768]{0:T(1024)} %get-tuple-element.57) | copy-start | bytes 9220
  960.0 70.6 %copy-start.70 = (f32[768]{0:T(1024)S(1)}, f32[768]{0:T(1024)}, u32[]{:S(2)}) copy-start(f32[768]{0:T(1024)} %get-tuple-element.70) | copy-start | bytes 9220
  (55 other events, 167.7 us)
Sparse Core Ops, SparseCore 0:
  13.8 47.6 all-gather.3
  297.6 43.3 reduce-scatter.4
  346.9 70.2 all-gather.5
  454.6 43.3 reduce-scatter.8
  500.7 43.3 reduce-scatter.6
  552.9 44.9 all-gather.7
  928.4 43.3 reduce-scatter.10
  978.8 252.8 all-reduce.4
